TPU v7x, 32 devices: a whole 2x2x4 slice. The times are simulated.
32 devices in a mesh: wide: 8 (over z, x), narrow: 4 (over y, core).
Axes of the slice: x: 2, y: 2, z: 4, core: 2. Of those that a mesh axis runs over, the one named last changes fastest.
Arguments:
- stream_one: bfloat16 [12288, 1024], P(('wide', 'narrow')), may hold values from -6 to 6
- stream_two: bfloat16 [12288, 1024], P(('wide', 'narrow')), may hold values from -6 to 6
- attention_gain: float32 [1024], replicated, may hold values from 0.5 to 1.5
- attention_shift: float32 [1024], replicated, may hold values from -1.8 to 1.8
- query_proj: bfloat16 [1024, 1024], P(None, 'narrow'), may hold values from -3.59375 to 3.59375
- value_proj: bfloat16 [1024, 1024], P(None, 'narrow'), may hold values from -0.1875 to 0.1875
- output_proj: bfloat16 [1024, 1024], P('narrow'), may hold values from -0.375 to 0.375
- forward_gain: float32 [1024], replicated, may hold values from 0.5 to 1.5
- forward_shift: float32 [1024], replicated, may hold values from -1.8 to 1.8
- up_proj: bfloat16 [1024, 4096], P(None, 'narrow'), may hold values from -0.1875 to 0.1875
- up_bias: float32 [4096], P('narrow'), may hold values from -1.8 to 1.8
- down_proj: bfloat16 [4096, 1024], P('narrow'), may hold values from -0.125 to 0.125
- down_bias: float32 [1024], replicated, may hold values from -1.8 to 1.8
- bucket_ids: int32 [12288, 4], P(('wide', 'narrow')), may hold values from 0 to 23
- sort_orders: int32 [8, 4, 1536], P('wide'), may hold values from 0 to 1535, as said below
- doc_lengths: int32 [8, 8], P('wide'), may hold values from 1 to 768, 1536 in all within a row
- cotan_one: bfloat16 [12288, 1024], P(('wide', 'narrow'))
- cotan_two: bfloat16 [12288, 1024], P(('wide', 'narrow'))
Outputs:
- output_one: bfloat16 [12288, 1024], P(('wide', 'narrow'))
- output_two: bfloat16 [12288, 1024], P(('wide', 'narrow'))
- grad_one: bfloat16 [12288, 1024], P(('wide', 'narrow'))
- grad_two: bfloat16 [12288, 1024], P(('wide', 'narrow'))
- grad_attention_gain: float32 [1024], replicated
- grad_attention_shift: float32 [1024], replicated
- grad_query_proj: float32 [1024, 1024], P(None, 'narrow')
- grad_value_proj: float32 [1024, 1024], P(None, 'narrow')
- grad_output_proj: float32 [1024, 1024], P('narrow')
- grad_forward_gain: float32 [1024], replicated
- grad_forward_shift: float32 [1024], replicated
- grad_up_proj: float32 [1024, 4096], P(None, 'narrow')
- grad_up_bias: float32 [4096], P('narrow')
- grad_down_proj: float32 [4096, 1024], P('narrow')
- grad_down_bias: float32 [1024], replicated
- bucket_counts: int32 [4, 24], replicated
Inputs may be any that keep to these rules, and one draw needn't show every extreme that they name: sort_orders[s, r] lists the 1536 positions of sequence s by increasing bucket of round r, ties by position. `doc_lengths`: the 8 documents of a sequence fill its 1536 positions in order.
All inputs are finite; a program needn't handle non-finite values.
Results may differ from a plain program's by a relative error of at most 0.019.
Values may be sent and summed in bfloat16 or wider, within the bound.
A program may use at most 256 MiB of HBM per device.

v0:
```python
import math
from types import SimpleNamespace

import jax
import jax.numpy as jnp
from jax import lax
from jax.experimental import pallas as pl
from jax.experimental.pallas import tpu as pltpu
from jax.sharding import PartitionSpec as P

HD = 128
GROUP = 64
NB = 24
MOST = 768
BLOCK = 256
LANES = 128
CHUNK = 128
NARROW = 4
VMEM_LIMIT = 60 << 20

FLOAT = jnp.float32
HALF = jnp.bfloat16
NEG = -1e30
EXP_SCALE = math.log2(math.e) / math.sqrt(HD)
FACTOR = 1.0 / math.sqrt(HD)
MESH = pl.DeviceIdType.MESH
IN_VMEM = pl.BlockSpec(memory_space=pltpu.VMEM)
IN_SMEM = pl.BlockSpec(memory_space=pltpu.SMEM)
ANYWHERE = pl.BlockSpec(memory_space=pl.ANY)
DMA = pltpu.SemaphoreType.DMA
WIDE = "wide"
DOCS = "docs"
FROM_HBM = "_any"


def normalize(inputs):
    center = inputs - jnp.mean(inputs, axis=-1, keepdims=True)
    inverse = lax.rsqrt(jnp.mean(center * center, axis=-1, keepdims=True) + 1e-05)
    return (center * inverse, inverse)


def norm_back(grad_out, scaled, inverse, gain):
    spread = grad_out * gain
    return inverse * (
        spread
        - jnp.mean(spread, axis=-1, keepdims=True)
        - scaled * jnp.mean(spread * scaled, axis=-1, keepdims=True)
    )


def contract_rows(left, right):
    return lax.dot_general(left, right, (((0,), (0,)), ((), ())), preferred_element_type=FLOAT)


def times_transpose(left, right):
    return lax.dot_general(left, right, (((1,), (1,)), ((), ())), preferred_element_type=FLOAT)


def times(left, right):
    return jnp.dot(left, right, preferred_element_type=FLOAT)


def column_sums(rows):
    return times(jnp.ones((8, rows.shape[0]), rows.dtype), rows)[0:1]


class Place:
    def __init__(self):
        index = lax.axis_index("narrow")
        core, chip = lax.rem(index, 2), lax.div(index, 2)
        self.me = index
        self.near = 2 * chip + 1 - core
        self.far = 2 * (1 - chip) + core
        self.cross = 2 * (1 - chip) + 1 - core


def span(start, size):
    return pl.ds(pl.multiple_of(start, size), size)


def remote(source, target, sent, arrived, other):
    return pltpu.make_async_remote_copy(
        src_ref=source,
        dst_ref=target,
        send_sem=sent,
        recv_sem=arrived,
        device_id={"narrow": other},
        device_id_type=MESH,
    )


class Gather:
    def __init__(self, place, whole, rows, sems):
        self.place, self.whole, self.rows = place, whole, rows
        self.sent, self.arrived = sems
        self.chunks = rows // CHUNK

    def at(self, owner, chunk):
        return self.whole.at[span(owner * self.rows + chunk * CHUNK, CHUNK), :]

    def copy(self, lane, owner, chunk, other):
        index = lane * self.chunks + chunk
        piece = self.at(owner, chunk)
        return remote(piece, piece, self.sent.at[index], self.arrived.at[index], other)

    def to_far(self, chunk):
        return self.copy(0, self.place.me, chunk, self.place.far)

    def to_near(self, chunk):
        return self.copy(1, self.place.me, chunk, self.place.near)

    def onward(self, chunk):
        return self.copy(2, self.place.far, chunk, self.place.near)

    def send(self, chunk):
        self.to_far(chunk).start()
        self.to_near(chunk).start()

    def take_near(self, chunk):
        self.to_near(chunk).wait_recv()

    def take_far(self, chunk):
        self.to_far(chunk).wait_recv()
        self.onward(chunk).start()

    def take_cross(self, chunk):
        self.onward(chunk).wait_recv()

    def finish(self):
        @pl.loop(0, self.chunks)
        def _(chunk):
            self.to_far(chunk).wait_send()
            self.to_near(chunk).wait_send()
            self.onward(chunk).wait_send()


class Scatter:
    def __init__(self, place, term, rows, buffers, sems):
        self.place, self.term, self.rows = place, term, rows
        self.near_out, self.near_in, self.far_out, self.far_in = buffers
        self.sent, self.arrived = sems
        self.chunks = rows // CHUNK

    def to_near(self, part, chunk):
        index = part * self.chunks + chunk
        at = span(chunk * CHUNK, CHUNK)
        return remote(
            self.near_out.at[part, at, :],
            self.near_in.at[part, at, :],
            self.sent.at[index],
            self.arrived.at[index],
            self.place.near,
        )

    def to_far(self, chunk):
        index = 2 * self.chunks + chunk
        at = span(chunk * CHUNK, CHUNK)
        return remote(
            self.far_out.at[at, :], self.far_in.at[at, :], self.sent.at[index], self.arrived.at[index], self.place.far
        )

    def part(self, owner, chunk):
        return self.term(span(owner * self.rows + chunk * CHUNK, CHUNK))

    def start(self, between=lambda: None):
        @pl.loop(0, self.chunks)
        def _(chunk):
            self.near_out[0, span(chunk * CHUNK, CHUNK), :] = self.part(self.place.cross, chunk).astype(HALF)
            self.to_near(0, chunk).start()

        between()

        @pl.loop(0, self.chunks)
        def _(chunk):
            at = span(chunk * CHUNK, CHUNK)
            own = self.part(self.place.far, chunk)
            self.to_near(0, chunk).wait_recv()
            self.far_out[at, :] = (own + self.near_in[0, at, :].astype(FLOAT)).astype(HALF)
            self.to_far(chunk).start()

        between()

        @pl.loop(0, self.chunks)
        def _(chunk):
            self.near_out[1, span(chunk * CHUNK, CHUNK), :] = self.part(self.place.near, chunk).astype(HALF)
            self.to_near(1, chunk).start()

    def chip_sum(self, chunk):
        own = self.part(self.place.me, chunk)
        self.to_near(1, chunk).wait_recv()
        return own + self.near_in[1, span(chunk * CHUNK, CHUNK), :].astype(FLOAT)

    def take_far(self, chunk):
        self.to_far(chunk).wait_recv()
        return self.far_in[span(chunk * CHUNK, CHUNK), :].astype(FLOAT)

    def finish(self):
        @pl.loop(0, self.chunks)
        def _(chunk):
            self.to_near(0, chunk).wait_send()
            self.to_near(1, chunk).wait_send()
            self.to_far(chunk).wait_send()


def pair_features(orders, docs, query_features, key_features, found):
    rounds, length = orders.shape
    groups = length // GROUP
    high_count = length // LANES
    high_rows = -(-high_count // 8) * 8
    count = docs.shape[0]
    depth = query_features.shape[0]
    lane = lax.broadcasted_iota(jnp.int32, (LANES, length), 1)
    low_at = lax.broadcasted_iota(jnp.int32, (LANES, length), 0)
    high_at = lax.broadcasted_iota(jnp.int32, (high_rows, length), 0)
    group_at = lax.broadcasted_iota(jnp.int32, (groups, LANES), 0).astype(FLOAT)
    sorted_group = lax.shift_right_logical(lane, int(math.log2(GROUP))).astype(FLOAT)

    @pl.loop(0, rounds)
    def _(index):
        row = orders[pl.ds(index, 1), :]
        high = jnp.where(high_at == lax.shift_right_logical(row, int(math.log2(LANES))), 1.0, 0.0)
        low = jnp.where(low_at == (row & (LANES - 1)), sorted_group, 0.0)
        found[index, :high_rows, :LANES] = times_transpose(high.astype(HALF), low.astype(HALF))
    place = lax.broadcasted_iota(jnp.int32, (count, LANES), 1)
    which = lax.broadcasted_iota(jnp.int32, (count, LANES), 0)
    begins = jnp.zeros((count, LANES), jnp.int32)
    ends = jnp.zeros((count, LANES), jnp.int32)
    begin = jnp.int32(0)
    for doc in range(count):
        end = begin + docs[doc]
        begins = jnp.where(which == doc, begin, begins)
        ends = jnp.where(which == doc, end, ends)
        begin = end
    rest = jnp.zeros((depth - rounds * groups - count, LANES), FLOAT)
    for block in range(high_count):
        mine, window = [], []
        for index in range(rounds):
            own = found[index, block : block + 1, :LANES]
            after = jnp.where(own == groups - 1.0, 0.0, own + 1.0)
            here = group_at == own
            mine.append(jnp.where(here, 1.0, 0.0))
            window.append(jnp.where(here | (group_at == after), 1.0, 0.0))
        at = place + block * LANES
        same = jnp.where((at >= begins) & (at < ends), 1.0, 0.0)
        lanes = slice(block * LANES, (block + 1) * LANES)
        query_features[:, lanes] = jnp.concatenate([*mine, same * (2.0 * rounds), rest], axis=0).astype(HALF)
        key_features[:, lanes] = jnp.concatenate([*window, same, rest], axis=0).astype(HALF)


def in_turn(place, step):
    flip_core, flip_chip = lax.rem(step, 2), lax.div(step, 2)
    core, chip = lax.rem(place.me, 2), lax.div(place.me, 2)
    core = core + flip_core * (1 - 2 * core)
    chip = chip + flip_chip * (1 - 2 * chip)
    return 2 * chip + core


def by_arrival(gather, act, after=None):
    place, rows = gather.place, gather.rows
    act(span(place.me * rows, rows))

    @pl.loop(0, gather.chunks)
    def _(chunk):
        gather.take_near(chunk)

    act(span(place.near * rows, rows))
    by_chunk(gather, act, after)


def by_chunk(gather, act, after=None):
    place, rows = gather.place, gather.rows

    @pl.loop(0, gather.chunks)
    def _(chunk):
        gather.take_far(chunk)
        if after is not None:
            pl.when(chunk == gather.chunks - 1)(after)
        act(span(place.far * rows + chunk * CHUNK, CHUNK))
        gather.take_cross(chunk)
        act(span(place.cross * rows + chunk * CHUNK, CHUNK))


def pair_bias(query_features, key_features, rounds, diagonal):
    counts = jnp.maximum(contract_rows(key_features, query_features) - 2.0 * rounds, 0.0)
    bias = jnp.where(counts > 0.0, jnp.log2(counts), NEG)
    if diagonal:
        key_at = lax.broadcasted_iota(jnp.int32, bias.shape, 0)
        query_at = lax.broadcasted_iota(jnp.int32, bias.shape, 1)
        bias = jnp.where(key_at < query_at, bias, NEG)
    return bias


def band_steps(length):
    return min(-(-(MOST - 1) // BLOCK), length // BLOCK - 1) + 1


def block_biases(block, steps, features, rounds, bias):
    query_features, key_features = features
    at = span(block * BLOCK, BLOCK)
    for step in range(steps):
        bias[step] = pair_bias(
            query_features[:, at], key_features[:, span((block - step) * BLOCK, BLOCK)], rounds, step == 0
        )


def attend(block, steps, rounds, queries, keys, values, features, merged, logs, bias, scores):
    at = span(block * BLOCK, BLOCK)
    heads = queries.shape[1] // HD
    block_biases(block, steps, features, rounds, bias)
    for head in range(heads):
        part = slice(head * HD, (head + 1) * HD)
        query = queries[at, part]
        peak = jnp.full((1, BLOCK), 2 * NEG, FLOAT)
        for step in range(steps):
            key_at = span((block - step) * BLOCK, BLOCK)
            score = times_transpose(keys[key_at, part], query) * EXP_SCALE + bias[step]
            scores[span((head * steps + step) * BLOCK, BLOCK), :] = score
            peak = jnp.maximum(peak, jnp.max(score, axis=0, keepdims=True))
        alone = peak < 0.5 * NEG
        peak = jnp.where(alone, 0.0, peak)
        total = jnp.zeros((1, BLOCK), FLOAT)
        mixed = jnp.zeros((HD, BLOCK), FLOAT)
        for step in range(steps):
            key_at = span((block - step) * BLOCK, BLOCK)
            powers = jnp.exp2(scores[span((head * steps + step) * BLOCK, BLOCK), :] - peak)
            total = total + jnp.sum(powers, axis=0, keepdims=True)
            mixed = mixed + contract_rows(values[key_at, part], powers.astype(HALF))
        total = jnp.where(alone, 1.0, total)
        mixed = jnp.where(alone, values[at, part].astype(FLOAT).T, mixed / total)
        merged[at, part] = mixed.T.astype(HALF)
        logs[head : head + 1, at] = jnp.where(alone, -NEG, peak + jnp.log2(total))


def attend_back(block, steps, rounds, queries, keys, values, features, grads, merged, logs, dq, dk, dv, bias):
    at = span(block * BLOCK, BLOCK)
    heads = queries.shape[1] // HD
    block_biases(block, steps, features, rounds, bias)
    ones = jnp.ones((8, HD), HALF)

    @pl.loop(0, heads)
    def _(head):
        part = span(head * HD, HD)
        query, grad = queries[at, part], grads[at, part]
        log_sum = logs[pl.ds(head, 1), at]
        product = grad.astype(FLOAT) * merged[at, part].astype(FLOAT)
        coarse = product.astype(HALF)
        fine = (product - coarse.astype(FLOAT)).astype(HALF)
        along = (times_transpose(ones, coarse) + times_transpose(ones, fine))[0:1]
        grad_query = jnp.zeros((HD, BLOCK), FLOAT)
        for step in range(steps):
            key_at = span((block - step) * BLOCK, BLOCK)
            key = keys[key_at, part]
            weights = jnp.exp2(times_transpose(key, query) * EXP_SCALE + bias[step] - log_sum)
            grad_probs = times_transpose(values[key_at, part], grad)
            grad_scores = (weights * (grad_probs - along)).astype(HALF)
            grad_value = times(weights.astype(HALF), grad)
            grad_key = times(grad_scores, query)
            if step == 0:
                dv[key_at, part] = grad_value
                dk[key_at, part] = grad_key
            else:
                dv[key_at, part] += grad_value
                dk[key_at, part] += grad_key
            grad_query = grad_query + contract_rows(key, grad_scores)
        dq[at, part] = grad_query.T


def finish_attention(queries, grads, logs, dq, dk, dv, grad_query, grad_value):
    length, width = queries.shape

    @pl.loop(0, length // BLOCK)
    def _(block):
        at = span(block * BLOCK, BLOCK)
        alone = jnp.where(logs[:, at] == -NEG, 1.0, 0.0).T
        for head in range(width // HD):
            part = slice(head * HD, (head + 1) * HD)
            grad_value[at, part] = (dv[at, part] + alone[:, head : head + 1] * grads[at, part].astype(FLOAT)).astype(HALF)
            query = queries[at, part].astype(FLOAT)
            key_scale = lax.rsqrt(jnp.sum(query * query, axis=-1, keepdims=True) + 1e-06)
            unit = query * key_scale
            grad_key = dk[at, part] * FACTOR
            key_along = jnp.sum(grad_key * unit, axis=-1, keepdims=True)
            grad_query[at, part] = (dq[at, part] * FACTOR + key_scale * (grad_key - unit * key_along)).astype(HALF)


def gelu_and_slope(hidden):
    square = hidden * hidden
    bend = jnp.tanh(math.sqrt(2.0 / math.pi) * hidden * (1.0 + 0.044715 * square))
    half_more = 0.5 + 0.5 * bend
    slope = half_more + 0.5 * hidden * (1.0 - bend * bend) * (
        math.sqrt(2.0 / math.pi) * (1.0 + 3.0 * 0.044715 * square)
    )
    return hidden * half_more, slope


def weight_grad(result, left, right, rows=None, add=False):
    width = 256
    height = result.shape[1] * result.shape[2] // right.shape[1]
    pieces = width // height
    rows = slice(None) if rows is None else rows

    @pl.loop(0, left.shape[1] // width)
    def _(index):
        block = contract_rows(left[rows, span(index * width, width)], right[rows, :])
        at = pl.ds(index * pieces, pieces)
        block = block.reshape(pieces, *result.shape[1:])
        if add:
            block = block + result[at].astype(FLOAT)
        result[at] = block.astype(result.dtype)


def ring_place(members, index):
    column, row = lax.rem(index, 2), lax.div(index, 2)
    return row + column * (members - 1 - 2 * row)


def ring_member(members, place):
    back = lax.div(place, members // 2)
    return 2 * place + back * (2 * (members - 1 - place) + 1 - 2 * place)


class Ring:
    def __init__(self, members, data, landed, result, sent, arrived, kept):
        self.members, self.data, self.landed, self.result = members, data, landed, result
        self.sent, self.arrived, self.kept, self.stage = sent, arrived, kept, 0
        self.here = ring_place(members, lax.axis_index("wide"))
        self.neighbours = (
            ring_member(members, lax.rem(self.here + 1, members)),
            ring_member(members, lax.rem(self.here + members - 1, members)),
        )

    def piece(self, direction, step):
        if direction == 0:
            return 2 * lax.rem(self.here - step + 2 * self.members, self.members)
        return 2 * lax.rem(self.here + step, self.members) + 1

    def copy(self, direction, step, at, gathering, fresh):
        index = direction * 2 * (self.members - 1) + step
        source = self.landed if gathering and not fresh else self.data
        return pltpu.make_async_remote_copy(
            src_ref=source.at[at],
            dst_ref=self.landed.at[at],
            send_sem=self.sent.at[index],
            recv_sem=self.arrived.at[index],
            device_id={"wide": self.neighbours[direction]},
            device_id_type=MESH,
        )

    def outgoing(self, direction, step, gathering=False, fresh=False):
        return self.copy(direction, step, self.piece(direction, step), gathering, fresh)

    def incoming(self, direction, step, gathering=False):
        return self.copy(direction, step, self.piece(direction, step + 1), gathering, False)

    def begin(self):
        for direction in range(2):
            self.outgoing(direction, 0).start()

    def add(self, direction, step):
        self.incoming(direction, step).wait_recv()
        at = self.piece(direction, step + 1)
        height = min(16, self.data.shape[1])

        @pl.loop(0, self.data.shape[1] // height)
        def _(index):
            rows = span(index * height, height)
            self.data[at, rows] = (
                self.data[at, rows].astype(FLOAT) + self.landed[at, rows].astype(FLOAT)
            ).astype(HALF)

        return at

    def keep(self, direction, step):
        at = self.piece(direction, step)
        source = self.data if isinstance(step, int) and step == self.members - 1 else self.landed
        return pltpu.make_async_copy(
            source.at[at], self.result.at[at], self.kept.at[direction * self.members + step - (self.members - 1)]
        )

    def advance(self):
        stage, last = self.stage, self.members - 1
        if stage == 14:
            return
        self.stage = stage + 1
        low, high = stage * 2 * last // 14, (stage + 1) * 2 * last // 14

        def repeat(begin, end, act):
            if end == begin + 1:
                act(begin)
            elif end > begin:
                pl.loop(begin, end)(act)

        def reduce(step):
            for direction in range(2):
                self.add(direction, step)
                self.outgoing(direction, step + 1).start()

        def forward(step):
            for direction in range(2):
                self.incoming(direction, step, True).wait_recv()
                self.outgoing(direction, step + 1, True).start()
                self.keep(direction, step + 1).start()

        repeat(low, min(high, last - 1), reduce)
        if low <= last - 1 < high:
            for direction in range(2):
                self.add(direction, last - 1)
                self.outgoing(direction, last, True, True).start()
                self.keep(direction, last).start()
        repeat(max(low, last), min(high, 2 * last - 1), forward)
        if low <= 2 * last - 1 < high:
            for direction in range(2):
                self.incoming(direction, 2 * last - 1, True).wait_recv()
                self.keep(direction, 2 * last).start()

    def finish(self):
        last = self.members - 1
        for direction in range(2):
            self.keep(direction, last).wait()
            self.outgoing(direction, last, True, True).wait_send()

        @pl.loop(0, last)
        def _(step):
            for direction in range(2):
                self.outgoing(direction, step).wait_send()

        @pl.loop(last + 1, 2 * last)
        def _(step):
            for direction in range(2):
                self.outgoing(direction, step, True).wait_send()
                self.keep(direction, step).wait()

        for direction in range(2):
            self.keep(direction, 2 * last).wait()


class Exchange:
    def __init__(self, members, data, landed, result, first, unit, bits, sems, stored):
        self.members, self.data, self.landed, self.result = members, data, landed, result
        self.first, self.unit, self.bits = first, unit, bits
        self.sent, self.arrived, self.stored, self.stage = *sems, stored, 0
        self.wide = lax.axis_index("wide")

    def bit(self, step):
        return lax.rem(lax.div(self.wide, 1 << self.bits[step]), 2)

    def size(self, step):
        return self.unit * (self.members >> (step + 1))

    def part(self, step, kept):
        start = self.first
        for before in range(step):
            start = start + self.bit(before) * self.size(before)
        bit = self.bit(step)
        return pl.ds(start + (bit if kept else 1 - bit) * self.size(step), self.size(step))

    def landing(self, step):
        return pl.ds(self.first + self.unit * self.members - 2 * self.size(step), self.size(step))

    def copy(self, step, gathering):
        index = step + gathering * len(self.bits)
        at = self.part(step, gathering)
        source = self.result if gathering and step < len(self.bits) - 1 else self.data
        return pltpu.make_async_remote_copy(
            src_ref=source.at[at],
            dst_ref=self.result.at[at] if gathering else self.landed.at[self.landing(step)],
            send_sem=self.sent.at[index],
            recv_sem=self.arrived.at[index],
            device_id={"wide": self.wide + (1 - 2 * self.bit(step)) * (1 << self.bits[step])},
            device_id_type=MESH,
        )

    def begin(self):
        self.copy(0, False).start()

    def advance(self):
        count, stage = len(self.bits), self.stage
        if stage == 2 * count:
            return
        self.stage = stage + 1
        if stage < count:
            self.copy(stage, False).wait_recv()
            kept, landed = self.part(stage, True), self.landing(stage)

            @pl.loop(0, self.size(stage))
            def _(index):
                at = kept.start + index
                self.data[at] = (
                    self.data[at].astype(FLOAT) + self.landed[landed.start + index].astype(FLOAT)
                ).astype(HALF)

        else:
            self.copy(2 * count - 1 - stage, True).wait_recv()
        if stage < count - 1:
            self.copy(stage + 1, False).start()
            return
        if stage == count - 1:
            self.store().start()
        if stage == count:
            self.store().wait()
        if stage < 2 * count - 1:
            self.copy(2 * count - 2 - stage, True).start()

    def store(self):
        at = self.part(len(self.bits) - 1, True)
        return pltpu.make_async_copy(self.data.at[at], self.result.at[at], self.stored)

    def finish(self):
        for step in range(len(self.bits)):
            self.copy(step, False).wait_send()
            self.copy(step, True).wait_send()


class Everyone:
    def __init__(self, axis, slots, sent, arrived):
        self.axis, self.slots, self.sent, self.arrived = axis, slots, sent, arrived
        self.me, self.members = lax.axis_index(axis), slots.shape[0]

    def copy(self, step):
        mine = self.slots.at[self.me]
        return pltpu.make_async_remote_copy(
            src_ref=mine,
            dst_ref=mine,
            send_sem=self.sent.at[step],
            recv_sem=self.arrived.at[step],
            device_id={self.axis: lax.rem(self.me + step, self.members)},
            device_id_type=MESH,
        )

    def send(self, value):
        self.slots[self.me] = value

        @pl.loop(1, self.members)
        def _(step):
            self.copy(step).start()

    def total(self):
        @pl.loop(1, self.members)
        def _(step):
            self.copy(step).wait()

        return lax.fori_loop(1, self.members, lambda index, total: total + self.slots[index], self.slots[0])


def advance(*exchanges):
    for exchange in exchanges:
        exchange.advance()


def greet_all(members):
    barrier = pltpu.get_barrier_semaphore()
    narrow, wide = lax.axis_index("narrow"), lax.axis_index("wide")

    @pl.loop(1, NARROW)
    def _(step):
        pl.semaphore_signal(
            barrier, inc=1, device_id={"narrow": lax.rem(narrow + step, NARROW)}, device_id_type=MESH
        )

    @pl.loop(1, members)
    def _(step):
        pl.semaphore_signal(barrier, inc=1, device_id={"wide": lax.rem(wide + step, members)}, device_id_type=MESH)

    return lambda: pl.semaphore_wait(barrier, NARROW - 1 + members - 1)


def layer(members, ref):
    place = Place()
    second_rows = ref.stream_two
    rows, width = second_rows.shape
    orders, docs = ref.orders, ref.docs
    rounds, length = orders.shape
    heads = ref.wq.shape[1]
    chunks = rows // CHUNK
    whole_one, whole_two, cotans, grad_rows = (ref.whole_one, ref.whole_two, ref.cotans, ref.grad_rows)
    queries, keys, values, merged, logs = (ref.queries, ref.keys, ref.values, ref.merged, ref.logs)
    features = (ref.query_features, ref.key_features)
    wq, wv, wo, up, down = (ref.wq, ref.wv, ref.wo, ref.up, ref.down)
    active, grad_hidden, middle, first_rows = (ref.active, ref.grad_hidden, ref.middle, ref.first_rows)
    grad_merged, bias, sums = ref.grad_merged, ref.bias, ref.sums
    dq, dk, dv = (ref.totals.at[pl.ds(i * length, length), :] for i in range(3))
    own_at, far_at = span(place.me * rows, rows), span(place.far * rows, rows)
    loads, stores = ref.loads, ref.stores

    def load(index, source, target):
        copy = pltpu.make_async_copy(source, target, loads.at[index])
        copy.start()
        return copy

    meet = greet_all(members)
    load_wq, load_wv = load(0, ref.wq_any, wq), load(1, ref.wv_any, wv)
    load_cotan = load(2, ref.cotan_two_any, cotans.at[own_at, :])
    load_wo, load_first = load(3, ref.wo_any, wo), load(4, ref.stream_one_any, first_rows)
    load_down, load_up = load(5, ref.down_any, down), load(6, ref.up_any, up)

    up_ring, down_ring = rings = [
        Ring(
            members, ref.sum_data[i], ref.sum_landed[i], ref.sum_results[i], ref.ring_sent.at[i], ref.ring_arrived.at[i],
            ref.ring_kept.at[i],
        )
        for i in range(2)
    ]
    bits = list(range(members.bit_length() - 1))
    swapped = bits[1::-1] + bits[2:]
    lanes = ((2, 0, bits), (2, members, swapped), (3, 0, bits), (3, members, swapped))
    out_sum, out_swap, in_sum, in_swap = exchanges = [
        Exchange(
            members, ref.sum_data[array], ref.sum_landed[array], ref.sum_results[array], first, 1, order,
            (ref.sum_sent.at[lane], ref.sum_arrived.at[lane]), ref.sum_stored.at[lane],
        )
        for lane, (array, first, order) in enumerate(lanes)
    ]
    queue = [up_ring, down_ring]

    def serve(*more):
        ring = queue.pop(0)
        queue.append(ring)
        advance(ring, *more)

    gather = Gather(place, whole_one, rows, (ref.gather_sent.at[0], ref.gather_arrived.at[0]))

    @pl.loop(0, chunks)
    def _(chunk):
        scaled, _ = normalize(second_rows[span(chunk * CHUNK, CHUNK), :].astype(FLOAT))
        normed = (scaled * ref.gain_one[...] + ref.shift_one[...]).astype(HALF)
        whole_one[span(place.me * rows + chunk * CHUNK, CHUNK), :] = normed

    meet()

    @pl.loop(0, chunks)
    def _(chunk):
        gather.send(chunk)

    pair_features(orders, docs, *features, bias)
    level = lax.broadcasted_iota(jnp.int32, (LANES, rows), 0)
    counted = jnp.ones((8, rows), HALF)
    sums[...] = jnp.zeros_like(sums)
    for index in range(rounds):
        found = jnp.where(level == ref.buckets[index : index + 1, :], 1.0, 0.0).astype(HALF)
        sums[4:5, index * LANES : (index + 1) * LANES] = times_transpose(counted, found)[0:1]
    load_wq.wait()
    load_wv.wait()

    def project(at):
        query = times(whole_one[at, :], wq[...]).astype(HALF)
        queries[at, :] = query
        for head in range(heads // HD):
            part = query[:, head * HD : (head + 1) * HD].astype(FLOAT)
            scale = lax.rsqrt(jnp.sum(part * part, axis=-1, keepdims=True) + 1e-06)
            keys[at, head * HD : (head + 1) * HD] = (part * scale).astype(HALF)
        values[at, :] = times(whole_one[at, :], wv[...]).astype(HALF)

    load_cotan.wait()
    spread = Gather(place, cotans, rows, (ref.gather_sent.at[1], ref.gather_arrived.at[1]))

    def send_cotangents():
        @pl.loop(0, chunks)
        def _(chunk):
            spread.send(chunk)

    by_arrival(gather, project, send_cotangents)
    gather.finish()

    steps = band_steps(length)
    blocks = length // BLOCK

    def forward(block, count):
        attend(block, count, rounds, queries, keys, values, features, merged, logs, bias, ref.totals)

    for block in range(steps - 1):
        forward(block, block + 1)

    @pl.loop(steps - 1, blocks)
    def _(block):
        forward(block, steps)

    buffers = (ref.near_out, ref.near_in, ref.far_out, ref.far_in)
    load_wo.wait()
    scatter = Scatter(
        place, lambda at: times(merged[at, :], wo[...]), rows, buffers, (ref.scatter_sent.at[0], ref.scatter_arrived.at[0])
    )
    scatter.start()
    load_first.wait()

    @pl.loop(0, chunks)
    def _(chunk):
        at = span(chunk * CHUNK, CHUNK)
        middle[at, :] = first_rows[at, :].astype(FLOAT) + scatter.chip_sum(chunk)

    @pl.loop(0, chunks)
    def _(chunk):
        spread.take_near(chunk)
        spread.take_far(chunk)

    load_down.wait()
    half_width = width // 2

    def grad_active(owner):
        @pl.loop(0, 2)
        def _(half):
            at = span(half * half_width, half_width)
            grad_hidden[span(owner * rows, rows), at] = times_transpose(
                cotans[span(owner * rows, rows), :], down[at, :]
            ).astype(HALF)

    @pl.loop(0, NARROW)
    def _(step):
        @pl.when(step == NARROW - 1)
        def _():
            @pl.loop(0, chunks)
            def _(chunk):
                spread.take_cross(chunk)

        grad_active(in_turn(place, step))

    gather = Gather(place, whole_two, rows, (ref.gather_sent.at[2], ref.gather_arrived.at[2]))
    load_up.wait()

    @pl.loop(0, chunks)
    def _(chunk):
        at = span(chunk * CHUNK, CHUNK)
        value = middle[at, :] + scatter.take_far(chunk)
        middle[at, :] = value
        first_rows[at, :] = value.astype(HALF)
        scaled, _ = normalize(value)
        whole_two[span(place.me * rows + chunk * CHUNK, CHUNK), :] = (
            scaled * ref.gain_two[...] + ref.shift_two[...]
        ).astype(HALF)
        gather.send(chunk)

    store_one = pltpu.make_async_copy(first_rows, ref.out_one, stores.at[0])
    store_one.start()

    def feed(row_at):
        @pl.loop(0, 2)
        def _(half):
            at = span(half * half_width, half_width)
            value, slope = gelu_and_slope(times(whole_two[row_at, :], up[:, at]) + ref.up_bias[:, at])
            active[row_at, at] = value.astype(HALF)
            grad_hidden[row_at, at] = (grad_hidden[row_at, at].astype(FLOAT) * slope).astype(HALF)

    chip = lax.div(place.me, 2)
    here, there = span(chip * 2 * rows, 2 * rows), span((1 - chip) * 2 * rows, 2 * rows)
    feed(span(place.me * rows, rows))

    @pl.loop(0, chunks)
    def _(chunk):
        gather.take_near(chunk)

    feed(span(place.near * rows, rows))
    weight_grad(ref.sum_data[1], active, cotans, here)
    weight_grad(ref.sum_data[0], whole_two, grad_hidden, here)
    by_chunk(gather, feed)
    scatter.finish()

    store_one.wait()
    load_cotan_one = load(7, ref.cotan_one_any, first_rows)
    scatter = Scatter(
        place,
        lambda at: times_transpose(grad_hidden[at, :], up[...]),
        rows,
        buffers,
        (ref.scatter_sent.at[1], ref.scatter_arrived.at[1]),
    )

    weight_grad(ref.sum_data[1], active, cotans, there, True)
    down_ring.begin()
    scatter.start()
    weight_grad(ref.sum_data[0], whole_two, grad_hidden, there, True)
    up_ring.begin()
    queue.reverse()
    back = Gather(place, grad_rows, rows, (ref.gather_sent.at[3], ref.gather_arrived.at[3]))
    load_cotan_one.wait()

    for chunk in range(chunks):
        at = span(chunk * CHUNK, CHUNK)
        grad_normed = scatter.chip_sum(chunk) + scatter.take_far(chunk)
        scaled, inverse = normalize(middle[at, :])
        grad = first_rows[at, :].astype(FLOAT) + norm_back(grad_normed, scaled, inverse, ref.gain_two[...])
        grad_rows[span(place.me * rows + chunk * CHUNK, CHUNK), :] = grad.astype(HALF)
        back.send(chunk)
        sums[2:3, :] += jnp.sum(grad_normed * scaled, axis=0, keepdims=True)
        sums[3:4, :] += jnp.sum(grad_normed, axis=0, keepdims=True)
        serve()
        serve()

    def merge_back(at):
        grad_merged[at, :] = times_transpose(grad_rows[at, :], wo[...]).astype(HALF)

    store_grad = pltpu.make_async_copy(grad_rows.at[own_at, :], ref.grad_one, stores.at[1])
    store_grad.start()
    own_sums = ref.wide_all.at[lax.axis_index(WIDE)]
    own_sums[5:6, :] = column_sums(grad_hidden[...])
    own_sums[6:7, :] = column_sums(cotans[...])
    scatter.finish()
    gather.finish()
    spread.finish()

    merge_back(span(place.me * rows, rows))
    serve()

    @pl.loop(0, chunks)
    def _(chunk):
        back.take_near(chunk)

    merge_back(span(place.near * rows, rows))
    serve()
    for chunk in range(chunks):
        back.take_far(chunk)
        merge_back(span(place.far * rows + chunk * CHUNK, CHUNK))
        back.take_cross(chunk)
        merge_back(span(place.cross * rows + chunk * CHUNK, CHUNK))
        serve()
    serve()
    weight_grad(ref.sum_data[2], merged, grad_rows)
    out_sum.begin()
    out_swap.begin()
    serve()

    fed = Scatter(
        place, lambda at: times(active[at, :], down[...]), rows, buffers, (ref.scatter_sent.at[2], ref.scatter_arrived.at[2])
    )
    fed.start()
    serve()

    def take_fed():
        @pl.loop(0, chunks)
        def _(chunk):
            at = span(chunk * CHUNK, CHUNK)
            total = fed.chip_sum(chunk) + fed.take_far(chunk) + ref.down_bias[...]
            cotans[span(place.near * rows + chunk * CHUNK, CHUNK), :] = (
                second_rows[at, :].astype(FLOAT) + total
            ).astype(HALF)

        store_two.start()
        fed.finish()
        for other in (place.near, place.far):
            pl.semaphore_signal(ref.ready, inc=1, device_id={"narrow": other}, device_id_type=MESH)

    store_two = pltpu.make_async_copy(cotans.at[span(place.near * rows, rows), :], ref.out_two, stores.at[2])

    for block in range(blocks):

        attend_back(
            block, min(block + 1, steps), rounds, queries, keys, values, features, grad_merged, merged, logs, dq, dk, dv, bias
        )
        serve()
        if block > 2:
            serve(out_sum, out_swap)
        if block == blocks - 2:
            take_fed()

    grad_query, grad_value = ref.grad_query, ref.grad_value
    finish_attention(queries, grad_merged, logs, dq, dk, dv, grad_query, grad_value)
    serve()
    weight_grad(ref.sum_data[3], whole_one, ref.grad_both)
    in_sum.begin()
    in_swap.begin()
    pl.semaphore_wait(ref.ready, 2)

    scatter = Scatter(
        place,
        lambda at: times_transpose(grad_query[at, :], wq[...]) + times_transpose(grad_value[at, :], wv[...]),
        rows,
        buffers,
        (ref.scatter_sent.at[3], ref.scatter_arrived.at[3]),
    )
    scatter.start()
    serve(out_sum, out_swap)
    serve(in_swap, in_sum)

    for chunk in range(chunks):
        at = span(chunk * CHUNK, CHUNK)
        grad_normed = scatter.chip_sum(chunk) + scatter.take_far(chunk)
        scaled, inverse = normalize(second_rows[at, :].astype(FLOAT))
        mine = span(place.me * rows + chunk * CHUNK, CHUNK)
        cotans[mine, :] = (
            cotans[mine, :].astype(FLOAT) + norm_back(grad_normed, scaled, inverse, ref.gain_one[...])
        ).astype(HALF)
        sums[0:1, :] += jnp.sum(grad_normed * scaled, axis=0, keepdims=True)
        sums[1:2, :] += jnp.sum(grad_normed, axis=0, keepdims=True)
        serve(*exchanges)
        serve()

    store_last = pltpu.make_async_copy(cotans.at[own_at, :], ref.grad_two, stores.at[3])
    store_last.start()
    over_narrow = Everyone("narrow", ref.narrow_all, ref.narrow_sent, ref.narrow_arrived)
    over_wide = Everyone("wide", ref.wide_all, ref.wide_sent, ref.wide_arrived)
    over_narrow.send(sums[...])
    serve(*exchanges)
    sums[...] = over_narrow.total()
    sums[5:7, :] = own_sums[5:7, :]
    over_wide.send(sums[...])
    while min(exchange.stage for exchange in exchanges) < 2 * len(bits) or min(ring.stage for ring in rings) < 14:
        serve(*exchanges)
    ref.small[...] = over_wide.total()
    scatter.finish()
    back.finish()
    for copy in (store_grad, store_two, store_last):
        copy.wait()
    for exchange in [*exchanges, *rings]:
        exchange.finish()


def pieces(members, shape):
    columns = shape[1] if members <= 8 else LANES
    return (2 * members, shape[0] * shape[1] // (2 * members * columns), columns)


def run_layer(members, args):
    rows, width = args.stream_two.shape
    length, heads, hidden = NARROW * rows, args.wq_any.shape[1], args.up_any.shape[1]
    rounds = args.orders.shape[0]
    chunks = rows // CHUNK
    depth = -(-(rounds * (length // GROUP) + args.docs.shape[0]) // LANES) * LANES
    weights = [(width, hidden), (hidden, width), (heads, width), (width, 2 * heads)]
    cut = [pieces(members, shape) for shape in weights]
    args = vars(args)
    in_specs = [IN_SMEM if k == DOCS else ANYWHERE if k.endswith(FROM_HBM) else IN_VMEM for k in args]
    outs = dict(
        out_one=((rows, width), HALF),
        out_two=((rows, width), HALF),
        grad_one=((rows, width), HALF),
        grad_two=((rows, width), HALF),
        small=((8, width), FLOAT),
    )
    out_shape = [jax.ShapeDtypeStruct(*o) for o in outs.values()] + [jax.ShapeDtypeStruct(shape, HALF) for shape in cut]
    out_specs = [ANYWHERE] * 4 + [IN_VMEM] + [ANYWHERE] * len(cut)
    tall = pltpu.VMEM((length, width), HALF)
    slim = pltpu.VMEM((length, heads), HALF)
    gather_sems, scatter_sems = DMA((4, 3 * chunks)), DMA((4, 3 * chunks))
    sum_sems = DMA((4, 2 * (members.bit_length() - 1)))
    ring_sems = DMA((2, 4 * (members - 1)))
    scratch = dict(
        whole_one=tall,
        whole_two=tall,
        cotans=tall,
        grad_rows=tall,
        active=pltpu.VMEM((length, hidden), HALF),
        grad_hidden=pltpu.VMEM((length, hidden), HALF),
        queries=slim,
        keys=slim,
        values=slim,
        merged=slim,
        grad_merged=slim,
        grad_both=pltpu.VMEM((length, 2 * heads), HALF),
        logs=pltpu.VMEM((8, length), FLOAT),
        query_features=pltpu.VMEM((depth, length), HALF),
        key_features=pltpu.VMEM((depth, length), HALF),
        wq=pltpu.VMEM((width, heads), HALF),
        wv=pltpu.VMEM((width, heads), HALF),
        wo=pltpu.VMEM((heads, width), HALF),
        up=pltpu.VMEM((width, hidden), HALF),
        down=pltpu.VMEM((hidden, width), HALF),
        middle=pltpu.VMEM((rows, width), FLOAT),
        first_rows=pltpu.VMEM((rows, width), HALF),
        bias=pltpu.VMEM((max(rounds, band_steps(length)), BLOCK, BLOCK), FLOAT),
        totals=pltpu.VMEM((3 * length, heads), FLOAT),
        sums=pltpu.VMEM((8, width), FLOAT),
        near_out=pltpu.VMEM((2, rows, width), HALF),
        near_in=pltpu.VMEM((2, rows, width), HALF),
        far_out=pltpu.VMEM((rows, width), HALF),
        far_in=pltpu.VMEM((rows, width), HALF),
        narrow_all=pltpu.VMEM((NARROW, 8, width), FLOAT),
        wide_all=pltpu.VMEM((members, 8, width), FLOAT),
        narrow_sent=DMA((NARROW,)),
        narrow_arrived=DMA((NARROW,)),
        wide_sent=DMA((members,)),
        wide_arrived=DMA((members,)),
        loads=DMA((8,)),
        stores=DMA((4,)),
        ready=pltpu.SemaphoreType.REGULAR,
        gather_sent=gather_sems,
        gather_arrived=gather_sems,
        scatter_sent=scatter_sems,
        scatter_arrived=scatter_sems,
        ring_sent=ring_sems,
        ring_arrived=ring_sems,
        ring_kept=DMA((2, 2 * members)),
        sum_sent=sum_sems,
        sum_arrived=sum_sems,
        sum_stored=DMA((4,)),
    )
    sum_buffers = [pltpu.VMEM(shape, HALF) for shape in cut]

    def kernel(*refs):
        count = len(args) + len(outs)
        named = dict(zip([*args, *outs], refs[:count]))
        results, rest = refs[count : count + len(cut)], refs[count + len(cut) :]
        named |= dict(zip(scratch, rest))
        rest = rest[len(scratch) :]
        ref = SimpleNamespace(**named, sum_results=results, sum_data=rest[: len(cut)], sum_landed=rest[len(cut) :])
        ref.grad_query = ref.grad_both.at[:, pl.ds(0, heads)]
        ref.grad_value = ref.grad_both.at[:, pl.ds(heads, heads)]
        layer(members, ref)

    found = pl.pallas_call(
        kernel,
        out_shape=out_shape,
        in_specs=in_specs,
        out_specs=out_specs,
        scratch_shapes=[*scratch.values(), *sum_buffers, *sum_buffers],
        compiler_params=pltpu.CompilerParams(collective_id=0, has_side_effects=True, vmem_limit_bytes=VMEM_LIMIT),
        name=layer.__name__,
    )(*args.values())
    sums = [result.reshape(shape) for result, shape in zip(found[len(outs) :], weights)]
    return SimpleNamespace(**dict(zip(outs, found))), sums


def finish(*refs):
    up, down, out, both, small, *rows = refs[:9]
    grad_up, grad_down, grad_out, grad_query, grad_value, *rest = refs[9:]
    heads = grad_query.shape[1]
    grad_up[...] = up[...].astype(FLOAT)
    grad_down[...] = down[...].astype(FLOAT)
    grad_out[...] = out[...].astype(FLOAT)
    grad_query[...] = both[:, :heads].astype(FLOAT)
    grad_value[...] = both[:, heads:].astype(FLOAT)
    for source, target in zip(rows, rest):
        target[...] = source[...]
    for source, target in zip((0, 1, 2, 3, 5, 6), rest[len(rows) :]):
        target[...] = small[source : source + 1, :]
    counts = rest[-1]
    for index in range(counts.shape[0]):
        counts[index : index + 1, :] = small[4:5, index * LANES : index * LANES + counts.shape[1]].astype(jnp.int32)


def run_finish(grads, small, rows, rounds):
    up, down, out, both = grads
    parts = 4
    vector = jax.ShapeDtypeStruct((1, small.shape[1]), FLOAT)
    taken = [up, down, out, both, small, *rows]
    given = [
        jax.ShapeDtypeStruct(up.shape, FLOAT),
        jax.ShapeDtypeStruct(down.shape, FLOAT),
        jax.ShapeDtypeStruct(out.shape, FLOAT),
        jax.ShapeDtypeStruct((both.shape[0], both.shape[1] // 2), FLOAT),
        jax.ShapeDtypeStruct((both.shape[0], both.shape[1] // 2), FLOAT),
        *[jax.ShapeDtypeStruct(r.shape, r.dtype) for r in rows],
        *[vector] * 6,
        jax.ShapeDtypeStruct((rounds, NB), jnp.int32),
    ]

    def spec(array):
        if array.shape[0] < LANES:
            return pl.BlockSpec(array.shape, lambda i: (0, 0))
        return pl.BlockSpec((array.shape[0] // parts, array.shape[1]), lambda i: (i, 0))

    return pl.pallas_call(
        finish,
        grid=(parts,),
        out_shape=given,
        in_specs=[spec(a) for a in taken],
        out_specs=[spec(a) for a in given],
        compiler_params=pltpu.CompilerParams(vmem_limit_bytes=VMEM_LIMIT),
        name=finish.__name__,
    )(*taken)


def per_device(
    stream_one,
    stream_two,
    attention_gain,
    attention_shift,
    query_proj,
    value_proj,
    output_proj,
    forward_gain,
    forward_shift,
    up_proj,
    up_bias,
    down_proj,
    down_bias,
    bucket_ids,
    sort_orders,
    doc_lengths,
    cotan_one,
    cotan_two,
):
    members = lax.axis_size("wide")
    row = lambda vector: vector.reshape(1, -1)
    found, grads = run_layer(
        members,
        SimpleNamespace(
            stream_one_any=stream_one,
            stream_two=stream_two,
            gain_one=row(attention_gain),
            shift_one=row(attention_shift),
            wq_any=query_proj,
            wv_any=value_proj,
            wo_any=output_proj,
            gain_two=row(forward_gain),
            shift_two=row(forward_shift),
            up_any=up_proj,
            up_bias=row(up_bias),
            down_any=down_proj,
            down_bias=row(down_bias),
            buckets=bucket_ids.T,
            orders=sort_orders[0],
            docs=doc_lengths[0],
            cotan_one_any=cotan_one,
            cotan_two_any=cotan_two,
        ),
    )
    rows = [found.out_one, found.out_two, found.grad_one, found.grad_two]
    grad_up, grad_down, grad_out, grad_query, grad_value, *rest = run_finish(
        grads, found.small, rows, sort_orders.shape[1]
    )
    gain_one, shift_one, gain_two, shift_two, bias_up, bias_down = [vector.reshape(-1) for vector in rest[4:10]]
    return (
        *rest[:4],
        gain_one,
        shift_one,
        grad_query,
        grad_value,
        grad_out,
        gain_two,
        shift_two,
        grad_up,
        bias_up,
        grad_down,
        bias_down,
        rest[10],
    )


def solution(mesh):
    rows = P(("wide", "narrow"), None)
    columns = P(None, "narrow")
    return jax.shard_map(
        per_device,
        mesh=mesh,
        in_specs=(
            rows,
            rows,
            P(),
            P(),
            columns,
            columns,
            P("narrow", None),
            P(),
            P(),
            columns,
            P("narrow"),
            P("narrow", None),
            P(),
            rows,
            P("wide", None, None),
            P("wide", None),
            rows,
            rows,
        ),
        out_specs=(
            rows,
            rows,
            rows,
            rows,
            P(),
            P(),
            columns,
            columns,
            P("narrow", None),
            P(),
            P(),
            columns,
            P("narrow"),
            P("narrow", None),
            P(),
            P(),
        ),
        check_vma=False,
    )
```

profile of v0, /device:TPU:0, one launch (start us, length us, event | category | flops | bytes accessed | tf_op | source)
XLA Modules:
  0.0 230.1 jit_solution(5569718151733357538)
XLA Ops:
  0.7 219.4 %layer.1 = (bf16[384,1024]{1,0:T(8,128)(2,1)}, bf16[384,1024]{1,0:T(8,128)(2,1)}, bf16[384,1024]{1,0:T(8,128)(2,1)}, bf16[384,1024]{1,0:T(8,128)(2,1)}, f32[8,10...) custom-call(bf16[384,1024]{1,0:T(8,128)(2,1)} %refs_0_.1, ...), custom_call_target="tpu_custom_call" | custom-call | tf_op jit(solution)/shard_map/layer/pallas_call | solution.py:1097
  220.0 9.9 %finish.1 = (f32[1024,1024]{1,0:T(8,128)}, f32[1024,1024]{1,0:T(8,128)}, f32[256,1024]{1,0:T(8,128)}, f32[1024,256]{1,0:T(8,128)}, f32[1024,256]{1,0:T(8,128)}, ...) custom-call(bf16[1024,1024]{1,0:T(8,128)(2,1)} %bitcast.19, ...), custom_call_target="tpu_custom_call" | custom-call | tf_op jit(solution)/shard_map/finish/pallas_call | solution.py:1149
where the time goes:
time: 230 us
  Pallas kernels  229 us (100%)
    pallas_call x1, Pallas kernels, run_layer(): pl.pallas_call(kernel, out_shape=out_shape, in_specs=in_specs, out_specs=...  219 us
    pallas_call x1, Pallas kernels, run_finish(): pl.pallas_call(finish, grid=(parts,), out_shape=given, in_specs=[spec(a)...  9.87 us

commit v1 on v0

--- a/solution.py
+++ b/solution.py
@@ -945,7 +945,7 @@
             block, min(block + 1, steps), rounds, queries, keys, values, features, grad_merged, merged, logs, dq, dk, dv, bias
         )
         serve()
-        if block > 2:
+        if block > 3:
             serve(out_sum, out_swap)
         if block == blocks - 2:
             take_fed()
@@ -967,7 +967,7 @@
     )
     scatter.start()
     serve(out_sum, out_swap)
-    serve(in_swap, in_sum)
+    serve()
 
     for chunk in range(chunks):
         at = span(chunk * CHUNK, CHUNK)
@@ -979,8 +979,8 @@
         ).astype(HALF)
         sums[0:1, :] += jnp.sum(grad_normed * scaled, axis=0, keepdims=True)
         sums[1:2, :] += jnp.sum(grad_normed, axis=0, keepdims=True)
-        serve(*exchanges)
-        serve()
+        serve(in_swap, in_sum)
+        serve(out_swap, out_sum)
 
     store_last = pltpu.make_async_copy(cotans.at[own_at, :], ref.grad_two, stores.at[3])
     store_last.start()
@@ -1127,7 +1127,7 @@
 
 def run_finish(grads, small, rows, rounds):
     up, down, out, both = grads
-    parts = 4
+    parts = 2
     vector = jax.ShapeDtypeStruct((1, small.shape[1]), FLOAT)
     taken = [up, down, out, both, small, *rows]
     given = [

time: 230 us -> 225 us (0.978)
  Pallas kernels: 229 us -> 224 us
    pallas_call x1, Pallas kernels: 219 us -> 216 us  [run_layer(): pl.pallas_call(kernel, out_shape=out_shape, in_specs=in_specs, out_specs=...]
where the time goes in v1:
time: 225 us
  Pallas kernels  224 us (100%)
    pallas_call x1, Pallas kernels, run_layer(): pl.pallas_call(kernel, out_shape=out_shape, in_specs=in_specs, out_specs=...  216 us
    pallas_call x1, Pallas kernels, run_finish(): pl.pallas_call(finish, grid=(parts,), out_shape=given, in_specs=[spec(a)...  8.74 us

profile of v1, /device:TPU:0, one launch (start us, length us, event | category | flops | bytes accessed | tf_op | source)
XLA Modules:
  0.0 225.1 jit_solution(15273708945623476639)
XLA Ops:
  0.7 215.5 %layer.1 = (bf16[384,1024]{1,0:T(8,128)(2,1)}, bf16[384,1024]{1,0:T(8,128)(2,1)}, bf16[384,1024]{1,0:T(8,128)(2,1)}, bf16[384,1024]{1,0:T(8,128)(2,1)}, f32[8,10...) custom-call(bf16[384,1024]{1,0:T(8,128)(2,1)} %refs_0_.1, ...), custom_call_target="tpu_custom_call" | custom-call | tf_op jit(solution)/shard_map/layer/pallas_call | solution.py:1097
  216.2 8.7 %finish.1 = (f32[1024,1024]{1,0:T(8,128)}, f32[1024,1024]{1,0:T(8,128)}, f32[256,1024]{1,0:T(8,128)}, f32[1024,256]{1,0:T(8,128)}, f32[1024,256]{1,0:T(8,128)}, ...) custom-call(bf16[1024,1024]{1,0:T(8,128)(2,1)} %bitcast.19, ...), custom_call_target="tpu_custom_call" | custom-call | tf_op jit(solution)/shard_map/finish/pallas_call | solution.py:1149
